TPU v7x, 512 devices: a whole 4x8x8 slice. The times are simulated.
512 devices in a mesh: row: 128 (over z, y_lo, x), ch: 4 (over y_hi, core).
Axes of the slice: x: 4, y: 8 (y_hi: 2, y_lo: 4; y = y_hi * 4 + y_lo), z: 8, core: 2. Of those that a mesh axis runs over, the one named last changes fastest.
Arguments:
- tokens: bfloat16 [384, 128, 512], P('row', None, 'ch'), may hold values from -6 to 6
- conv_weight: float32 [7, 7, 512], P(None, None, 'ch'), may hold values from -0.875 to 0.875
- spectral_filter: bfloat16 [2, 384, 128, 512], P(None, None, 'row', 'ch'), may hold values from -5 to 5
- cotangent: bfloat16 [384, 128, 512], P('row', None, 'ch'), may hold values from -6 to 6
Outputs:
- filtered: bfloat16 [384, 128, 512], P('row', None, 'ch')
- token_grad: bfloat16 [384, 128, 512], P('row', None, 'ch')
- filter_grad: float32 [2, 384, 128, 512], P(None, None, 'row', 'ch')
- conv_grad: float32 [7, 7, 512], P(None, None, 'ch')
All inputs are finite; a program needn't handle non-finite values.
Results may differ from a plain program's by a relative error of at most 0.005.
Values may be sent and summed in bfloat16 or wider, within the bound.
A program may use at most 64 MiB of HBM per device.

v0:
```python
import math
import jax
import jax.numpy as jnp
from jax import lax
from jax.sharding import PartitionSpec as P

HIGHEST = lax.Precision.HIGHEST


def extended(block, sides, width):
    for axis, dim in sides:
        count = lax.axis_size(axis)
        forward = [(i, i + 1) for i in range(count - 1)]
        backward = [(target, source) for source, target in forward]
        low = lax.ppermute(
            lax.slice_in_dim(block, block.shape[dim] - width, None, axis=dim), axis, forward
        )
        high = lax.ppermute(lax.slice_in_dim(block, 0, width, axis=dim), axis, backward)
        block = jnp.concatenate([low, block, high], axis=dim)
    return block


def tables(length):
    index = jnp.arange(length, dtype=jnp.int32)
    product = index[:, None] * index[None, :] % length
    angle = product.astype(jnp.float32) * (2.0 * math.pi / length)
    return (jnp.cos(angle), jnp.sin(angle))


def depthwise(padded, weight, row_count, col_count):
    total = jnp.zeros((row_count, col_count, weight.shape[2]), jnp.float32)
    for shift_row in range(7):
        for shift_col in range(7):
            total = (
                total
                + weight[shift_row, shift_col]
                * padded[shift_row : shift_row + row_count, shift_col : shift_col + col_count]
            )
    return total


def along_cols(field, table):
    return jnp.einsum("rwc,wk->rkc", field, table, precision=HIGHEST)


def along_rows(table, field):
    return jnp.einsum("kh,hlc->klc", table, field, precision=HIGHEST)


def to_spectrum(real_part, imag_part, cosine_rows, sine_rows):
    out_re = along_rows(cosine_rows, real_part) + along_rows(sine_rows, imag_part)
    out_im = along_rows(cosine_rows, imag_part) - along_rows(sine_rows, real_part)
    return (out_re, out_im)


def from_spectrum(real_part, imag_part, cosine_rows, sine_rows):
    out_re = along_rows(cosine_rows, real_part) - along_rows(sine_rows, imag_part)
    out_im = along_rows(cosine_rows, imag_part) + along_rows(sine_rows, real_part)
    return (out_re, out_im)


def weight_terms(field_grad, padded, row_count, col_count):
    return jnp.stack(
        [
            jnp.stack(
                [
                    jnp.sum(field_grad * padded[a : a + row_count, b : b + col_count], axis=(0, 1))
                    for b in range(7)
                ]
            )
            for a in range(7)
        ]
    )


def row_tiles(tokens, conv_weight, spectral_filter, cotangent):
    row_count, col_count, chan_count = tokens.shape
    height = row_count * lax.axis_size("row")
    inverse_count = 1.0 / (height * col_count)
    cosine_cols, sine_cols = tables(col_count)
    cosine_rows, sine_rows = tables(height)
    token_rim = extended(tokens, (("row", 0),), 3)
    padded = jnp.pad(token_rim.astype(jnp.float32), ((0, 0), (3, 3), (0, 0)))
    conv_out = depthwise(padded, conv_weight, row_count, col_count)
    field_re = along_cols(conv_out, cosine_cols)
    field_im = -along_cols(conv_out, sine_cols)
    cot_float = cotangent.astype(jnp.float32)
    cot_re = along_cols(cot_float, cosine_cols)
    cot_im = -along_cols(cot_float, sine_cols)
    filt_re = spectral_filter[0].astype(jnp.float32)
    filt_im = spectral_filter[1].astype(jnp.float32)
    slab_re, slab_im = (
        lax.all_to_all(field_re, "row", split_axis=1, concat_axis=0, tiled=True),
        lax.all_to_all(field_im, "row", split_axis=1, concat_axis=0, tiled=True),
    )
    spec_re, spec_im = to_spectrum(slab_re, slab_im, cosine_rows, sine_rows)
    prod_re = filt_re * spec_re - filt_im * spec_im
    prod_im = filt_re * spec_im + filt_im * spec_re
    inv_re, inv_im = from_spectrum(prod_re, prod_im, cosine_rows, sine_rows)
    tile_re, tile_im = (
        lax.all_to_all(inv_re, "row", split_axis=0, concat_axis=1, tiled=True),
        lax.all_to_all(inv_im, "row", split_axis=0, concat_axis=1, tiled=True),
    )
    cslab_re, cslab_im = (
        lax.all_to_all(cot_re, "row", split_axis=1, concat_axis=0, tiled=True),
        lax.all_to_all(cot_im, "row", split_axis=1, concat_axis=0, tiled=True),
    )
    grad_re, grad_im = to_spectrum(cslab_re, cslab_im, cosine_rows, sine_rows)
    grad_re = grad_re * inverse_count
    grad_im = grad_im * inverse_count
    back_re = grad_re * filt_re + grad_im * filt_im
    back_im = grad_im * filt_re - grad_re * filt_im
    ginv_re, ginv_im = from_spectrum(back_re, back_im, cosine_rows, sine_rows)
    gtile_re, gtile_im = (
        lax.all_to_all(ginv_re, "row", split_axis=0, concat_axis=1, tiled=True),
        lax.all_to_all(ginv_im, "row", split_axis=0, concat_axis=1, tiled=True),
    )
    filter_grad = jnp.stack(
        [grad_re * spec_re + grad_im * spec_im, grad_im * spec_re - grad_re * spec_im]
    )
    filtered = (
        (along_cols(tile_re, cosine_cols) - along_cols(tile_im, sine_cols)) * inverse_count
    ).astype(jnp.bfloat16)
    field_grad = along_cols(gtile_re, cosine_cols) - along_cols(gtile_im, sine_cols)
    grad_rim = extended(field_grad, (("row", 0),), 3)
    grad_pad = jnp.pad(grad_rim, ((0, 0), (3, 3), (0, 0)))
    token_grad = depthwise(grad_pad, conv_weight[::-1, ::-1], row_count, col_count).astype(
        jnp.bfloat16
    )
    partial_grad = weight_terms(field_grad, padded, row_count, col_count)
    conv_grad = lax.psum(partial_grad, "row") / math.sqrt(height * col_count)
    return (filtered, token_grad, filter_grad, conv_grad)


def per_device(tokens, conv_weight, spectral_filter, cotangent):
    return row_tiles(tokens, conv_weight, spectral_filter, cotangent)


def solution(mesh):
    in_specs = (
        P("row", None, "ch"),
        P(None, None, "ch"),
        P(None, None, "row", "ch"),
        P("row", None, "ch"),
    )
    out_specs = (
        P("row", None, "ch"),
        P("row", None, "ch"),
        P(None, None, "row", "ch"),
        P(None, None, "ch"),
    )
    return jax.shard_map(
        per_device, mesh=mesh, in_specs=in_specs, out_specs=out_specs, check_vma=False
    )
```

profile of v0, /device:TPU:40, one launch (start us, length us, event | category | flops | bytes accessed | tf_op | source)
XLA Modules:
  0.0 941.6 jit_solution(396163082504076539)
XLA Ops:
  0.6 0.0 copy-start
  0.6 3.5 collective-permute-start
  4.2 4.6 collective-permute-start.1
  8.8 0.5 fusion.4
  9.2 0.8 copy.29
  10.1 17.0 %all-to-all-start.5 = ((f32[3,128,128]{2,0,1:T(4,128)}), f32[3,128,128]{2,0,1:T(4,128)S(1)}, u32[]{:S(2)}, u32[]{:S(2)}) async-start(f32[3,128,128]{2,0,1:T(4,128)} %copy.29), calls=%async_computation.5 | async-start | bytes 524288 | tf_op jit(solution)/shard_map/all_to_all | solution.py:106
  27.1 0.5 convolution_bitcast_fusion
  27.6 0.0 copy-start.1
  27.6 0.8 copy.28
  28.5 0.0 copy-done.1
  28.6 1.0 multiply_add_fusion
  29.6 0.6 convolution_bitcast_fusion.1
  30.1 0.8 copy.22
  31.0 9.1 all-to-all-done.5
  40.1 7.2 all-to-all-start.4
  47.2 0.6 fusion.5
  47.8 0.8 copy.23
  48.6 0.1 reshape.105
  48.7 3.6 fusion.19
  52.3 8.1 all-to-all-done.4
  60.4 7.5 all-to-all-start
  67.9 0.1 reshape.104
  68.0 3.6 fusion.21
  71.6 3.6 fusion.3
  75.2 0.0 copy-start.3
  75.2 3.6 fusion.2
  78.8 2.9 fusion.15
  81.8 3.6 convolution_add_fusion
  85.4 14.5 %all-to-all-start.1 = ((f32[3,128,128]{2,0,1:T(4,128)}), f32[3,128,128]{2,0,1:T(4,128)S(1)}, u32[]{:S(2)}, u32[]{:S(2)}) async-start(f32[3,128,128]{2,0,1:T(4,128)} %copy.23), calls=%async_computation.1 | async-start | bytes 524288 | tf_op jit(solution)/shard_map/all_to_all | solution.py:94
  99.9 2.9 fusion.17
  102.9 3.6 convolution_subtract_fusion.1
  106.5 0.1 reshape.102
  106.6 6.0 all-to-all-done.1
  112.6 8.1 all-to-all-start.6
  120.7 0.1 reshape.103
  120.8 3.6 fusion.27
  124.4 3.6 fusion.29
  128.0 3.6 convolution_subtract_fusion.5
  131.6 4.0 convolution_add_fusion.3
  135.6 2.9 fusion.23
  138.5 3.6 convolution_add_fusion.2
  142.2 2.9 fusion.25
  145.2 14.4 %all-to-all-start.7 = ((f32[384,1,128]{2,1,0:T(1,128)}), f32[384,1,128]{2,1,0:T(1,128)S(1)}, u32[]{:S(2)}, u32[]{:S(2)}) async-start(f32[384,1,128]{2,1,0:T(1,128)} %bitcast.84), calls=%async_computation.7 | async-start | bytes 393216 | tf_op jit(solution)/shard_map/all_to_all | solution.py:116
  159.6 3.6 convolution_subtract_fusion.4
  163.2 0.8 pad_maximum_fusion
  164.0 0.6 fusion.147
  164.5 7.2 all-to-all-done.7
  171.8 6.9 all-to-all-start.2
  178.6 0.6 multiply_reduce_fusion.48
  179.2 0.2 multiply_reduce_fusion.19
  179.5 0.2 multiply_reduce_fusion.39
  179.7 0.2 multiply_reduce_fusion.29
  179.9 0.2 multiply_reduce_fusion.1
  180.2 0.2 multiply_reduce_fusion
  180.4 4.6 collective-permute-start.3
  185.0 1.9 collective-permute-start.2
  187.2 713.5 %psum.7 = f32[7,7,128]{2,1,0:T(8,128)S(1)} all-reduce(f32[7,7,128]{2,1,0:T(8,128)S(1)} %constant_dynamic-update-slice_fusion), channel_id=1, replica_groups=mesh['row'=128,'ch'=4] {'row'}, use_global_device_ids=true, to_apply=%region_49.50 | all-reduce | flops 6272 | bytes 50176 | tf_op jit(solution)/shard_map/psum | solution.py:131
  900.7 25.3 %all-to-all-start.3 = ((f32[384,1,128]{2,1,0:T(1,128)}), f32[384,1,128]{2,1,0:T(1,128)S(1)}, u32[]{:S(2)}, u32[]{:S(2)}) async-start(f32[384,1,128]{2,1,0:T(1,128)} %bitcast.67), calls=%async_computation.3 | async-start | bytes 393216 | tf_op jit(solution)/shard_map/all_to_all | solution.py:102
  926.1 0.6 broadcast_multiply_fusion
  926.7 0.6 fusion.150
  927.3 11.2 %all-to-all-done.3 = f32[384,1,128]{2,1,0:T(1,128)S(1)} async-done(((f32[384,1,128]{2,1,0:T(1,128)}), f32[384,1,128]{2,1,0:T(1,128)S(1)}, u32[]{:S(2)}, u32[]{:S(2)}) %all-to-all-start.3) | async-done | bytes 196640 | tf_op jit(solution)/shard_map/all_to_all | solution.py:102
  938.4 1.2 fusion.7
  939.6 0.1 select_maximum_fusion
  939.7 1.7 fusion.156
  (30 shorter events, 0.4 us)
Async XLA Ops:
  0.6 8.1 copy-start
  0.6 27.8 %collective-permute-start = (bf16[3,128,128]{2,1,0:T(8,128)(2,1)}, bf16[3,128,128]{2,1,0:T(8,128)(2,1)S(1)}, u32[]{:S(2)}, u32[]{:S(2)}) collective-permute-start(bf16[3,128,128]{2,1,0:T(8,128)(2,1)} %param.4), channel_id=1, source_target_pairs={{0,4},{4,8},{8,12},{12,16},{16,20},{20,24},{24,28},{28,32},{32,36}... | collective-permute-start | bytes 294920 | tf_op jit(solution)/shard_map/ppermute | solution.py:15
  4.2 24.3 %collective-permute-start.1 = (bf16[3,128,128]{2,1,0:T(8,128)(2,1)}, bf16[3,128,128]{2,1,0:T(8,128)(2,1)S(1)}, u32[]{:S(2)}, u32[]{:S(2)}) collective-permute-start(bf16[3,128,128]{2,1,0:T(8,128)(2,1)} %param.4), channel_id=1, source_target_pairs={{4,0},{8,4},{12,8},{16,12},{20,16},{24,20},{28,24},{32,28},{36,32}... | collective-permute-start | bytes 294920 | tf_op jit(solution)/shard_map/ppermute | solution.py:18
  10.1 17.0 %copy-start.2 = (f32[7,7,128]{2,1,0:T(8,128)S(1)}, f32[7,7,128]{2,1,0:T(8,128)}, u32[]{:S(2)}) copy-start(f32[7,7,128]{2,1,0:T(8,128)} %param.5) | copy-start | bytes 75268
  10.1 30.0 %all-to-all-start.5 = ((f32[3,128,128]{2,0,1:T(4,128)}), f32[3,128,128]{2,0,1:T(4,128)S(1)}, u32[]{:S(2)}, u32[]{:S(2)}) async-start(f32[3,128,128]{2,0,1:T(4,128)} %copy.29), calls=%async_computation.5 | async-start | bytes 524288 | tf_op jit(solution)/shard_map/all_to_all | solution.py:106
  27.6 0.9 copy-start.1
  40.1 20.4 %all-to-all-start.4 = ((f32[3,128,128]{2,0,1:T(4,128)}), f32[3,128,128]{2,0,1:T(4,128)S(1)}, u32[]{:S(2)}, u32[]{:S(2)}) async-start(f32[3,128,128]{2,0,1:T(4,128)} %copy.28), calls=%async_computation.4 | async-start | bytes 524288 | tf_op jit(solution)/shard_map/all_to_all | solution.py:105
  60.4 25.0 %all-to-all-start = ((f32[3,128,128]{2,0,1:T(4,128)}), f32[3,128,128]{2,0,1:T(4,128)S(1)}, u32[]{:S(2)}, u32[]{:S(2)}) async-start(f32[3,128,128]{2,0,1:T(4,128)} %copy.22), calls=%async_computation | async-start | bytes 524288 | tf_op jit(solution)/shard_map/all_to_all | solution.py:93
  75.2 3.6 copy-start.3
  85.4 27.2 %all-to-all-start.1 = ((f32[3,128,128]{2,0,1:T(4,128)}), f32[3,128,128]{2,0,1:T(4,128)S(1)}, u32[]{:S(2)}, u32[]{:S(2)}) async-start(f32[3,128,128]{2,0,1:T(4,128)} %copy.23), calls=%async_computation.1 | async-start | bytes 524288 | tf_op jit(solution)/shard_map/all_to_all | solution.py:94
  112.6 32.6 %all-to-all-start.6 = ((f32[384,1,128]{2,1,0:T(1,128)}), f32[384,1,128]{2,1,0:T(1,128)S(1)}, u32[]{:S(2)}, u32[]{:S(2)}) async-start(f32[384,1,128]{2,1,0:T(1,128)} %bitcast.79), calls=%async_computation.6 | async-start | bytes 393216 | tf_op jit(solution)/shard_map/all_to_all | solution.py:115
  145.2 26.6 %all-to-all-start.7 = ((f32[384,1,128]{2,1,0:T(1,128)}), f32[384,1,128]{2,1,0:T(1,128)S(1)}, u32[]{:S(2)}, u32[]{:S(2)}) async-start(f32[384,1,128]{2,1,0:T(1,128)} %bitcast.84), calls=%async_computation.7 | async-start | bytes 393216 | tf_op jit(solution)/shard_map/all_to_all | solution.py:116
  171.8 729.0 %all-to-all-start.2 = ((f32[384,1,128]{2,1,0:T(1,128)}), f32[384,1,128]{2,1,0:T(1,128)S(1)}, u32[]{:S(2)}, u32[]{:S(2)}) async-start(f32[384,1,128]{2,1,0:T(1,128)} %bitcast.62), calls=%async_computation.2 | async-start | bytes 393216 | tf_op jit(solution)/shard_map/all_to_all | solution.py:101
  180.4 759.2 %collective-permute-start.3 = (f32[3,128,128]{2,1,0:T(8,128)S(1)}, f32[3,128,128]{2,1,0:T(8,128)S(1)}, u32[]{:S(2)}, u32[]{:S(2)}) collective-permute-start(f32[3,128,128]{2,1,0:T(8,128)S(1)} %get-tuple-element.116), channel_id=1, source_target_pairs={{4,0},{8,4},{12,8},{16,12},{20,16},{24,20},{28,24},{32,28},{36,32}... | collective-permute-start | bytes 589832 | tf_op jit(solution)/shard_map/ppermute | solution.py:18
  185.0 754.6 %collective-permute-start.2 = (f32[3,128,128]{2,1,0:T(8,128)S(1)}, f32[3,128,128]{2,1,0:T(8,128)S(1)}, u32[]{:S(2)}, u32[]{:S(2)}) collective-permute-start(f32[3,128,128]{2,1,0:T(8,128)S(1)} %get-tuple-element.116), channel_id=1, source_target_pairs={{0,4},{4,8},{8,12},{12,16},{16,20},{20,24},{24,28},{28,32},{32,36}... | collective-permute-start | bytes 589832 | tf_op jit(solution)/shard_map/ppermute | solution.py:15
  900.7 37.7 %all-to-all-start.3 = ((f32[384,1,128]{2,1,0:T(1,128)}), f32[384,1,128]{2,1,0:T(1,128)S(1)}, u32[]{:S(2)}, u32[]{:S(2)}) async-start(f32[384,1,128]{2,1,0:T(1,128)} %bitcast.67), calls=%async_computation.3 | async-start | bytes 393216 | tf_op jit(solution)/shard_map/all_to_all | solution.py:102
where the time goes:
time: 950 us; the launch traced here: 942 us
  blocking collectives  714 us (75%)
  starting transfers between devices  115 us (12%)
  matrix products  60.5 us (6%)
  waiting for transfers between devices  41.6 us (4%)
    psum x1, blocking collectives, row_tiles(): conv_grad = lax.psum(partial_grad, 'row') / math.sqrt(height * col_count)  714 us
    dot_general x16, matrix products, along_rows(): return jnp.einsum('kh,hlc->klc', table, field, precision=HIGHEST)  55.5 us
    all_to_all x1, starting transfers between devices, row_tiles(): lax.all_to_all(inv_im, 'row', split_axis=0, concat_axis=1, tiled=True)  25.3 us
  transfers between devices with their start and end apart: 12, of which 5 were waited for; matrix products, arithmetic and copies ran while one was open for 7% of the time, Pallas kernels for 0%

commit v1 on v0

--- a/solution.py
+++ b/solution.py
@@ -1,3 +1,4 @@
+import functools
 import math
 import jax
 import jax.numpy as jnp
@@ -5,6 +6,15 @@
 from jax.sharding import PartitionSpec as P
 
 HIGHEST = lax.Precision.HIGHEST
+
+
+def take_zones(t0, along_axis):
+    block_now = jax.lax.all_gather(t0, along_axis)
+    prior = jnp.sum(block_now, axis=0)
+    return prior
+
+
+target_lay = functools.partial(take_zones, along_axis="row")
 
 
 def extended(block, sides, width):
@@ -128,7 +138,7 @@
         jnp.bfloat16
     )
     partial_grad = weight_terms(field_grad, padded, row_count, col_count)
-    conv_grad = lax.psum(partial_grad, "row") / math.sqrt(height * col_count)
+    conv_grad = target_lay(partial_grad) / math.sqrt(height * col_count)
     return (filtered, token_grad, filter_grad, conv_grad)
 
 

time: 950 us -> 829 us (0.87)
  the two profiles are of different devices: /device:TPU:40 before, /device:TPU:32 now
where the time goes in v1:
time: 829 us; the launch traced here: 824 us
  waiting for transfers between devices  652 us (79%)
  starting transfers between devices  84.3 us (10%)
  matrix products  60.1 us (7%)
  between operations  14.7 us (2%)
    all_gather x1, waiting for transfers between devices, take_zones(): block_now = jax.lax.all_gather(t0, along_axis)  582 us
    dot_general x16, matrix products, along_rows(): return jnp.einsum('kh,hlc->klc', table, field, precision=HIGHEST)  55.1 us
  transfers between devices with their start and end apart: 13, of which 9 were waited for; matrix products, arithmetic and copies ran while one was open for 8% of the time, Pallas kernels for 0%

profile of v1, /device:TPU:32, one launch (start us, length us, event | category | flops | bytes accessed | tf_op | source)
XLA Modules:
  0.0 824.3 jit_solution(9178410229995093467)
XLA Ops:
  7.2 0.9 copy-done
  8.1 0.5 convolution_bitcast_fusion
  8.5 0.8 copy.28
  9.4 15.3 %all-to-all-start.4 = ((f32[3,128,128]{2,0,1:T(4,128)}), f32[3,128,128]{2,0,1:T(4,128)S(1)}, u32[]{:S(2)}, u32[]{:S(2)}) async-start(f32[3,128,128]{2,0,1:T(4,128)} %copy.28), calls=%async_computation.4 | async-start | bytes 524288 | tf_op jit(solution)/shard_map/all_to_all | solution.py:115
  24.7 0.5 fusion.4
  25.2 0.8 copy.29
  26.0 13.3 %all-to-all-done.4 = f32[3,128,128]{2,0,1:T(4,128)S(1)} async-done(((f32[3,128,128]{2,0,1:T(4,128)}), f32[3,128,128]{2,0,1:T(4,128)S(1)}, u32[]{:S(2)}, u32[]{:S(2)}) %all-to-all-start.4) | async-done | bytes 196640 | tf_op jit(solution)/shard_map/all_to_all | solution.py:115
  39.4 6.2 all-to-all-start.5
  45.5 1.3 collective-permute-start.1
  46.8 4.7 collective-permute-start
  51.6 0.1 reshape.104
  51.7 3.6 fusion.21
  55.3 4.3 all-to-all-done.5
  59.6 3.6 fusion.19
  63.2 3.6 fusion.2
  66.8 3.6 fusion.3
  70.5 2.9 fusion.17
  73.4 3.6 convolution_subtract_fusion.1
  77.1 14.5 %all-to-all-start.6 = ((f32[384,1,128]{2,1,0:T(1,128)}), f32[384,1,128]{2,1,0:T(1,128)S(1)}, u32[]{:S(2)}, u32[]{:S(2)}) async-start(f32[384,1,128]{2,1,0:T(1,128)} %bitcast.79), calls=%async_computation.6 | async-start | bytes 393216 | tf_op jit(solution)/shard_map/all_to_all | solution.py:125
  91.6 2.9 fusion.15
  94.5 3.6 convolution_add_fusion
  98.2 5.8 all-to-all-done.6
  104.0 8.4 %all-to-all-start.7 = ((f32[384,1,128]{2,1,0:T(1,128)}), f32[384,1,128]{2,1,0:T(1,128)S(1)}, u32[]{:S(2)}, u32[]{:S(2)}) async-start(f32[384,1,128]{2,1,0:T(1,128)} %bitcast.84), calls=%async_computation.7 | async-start | bytes 393216 | tf_op jit(solution)/shard_map/all_to_all | solution.py:126
  112.4 0.4 all-gather.3.cloned.1.call-start
  112.9 0.6 fusion.147
  113.5 11.3 %all-to-all-done.7 = f32[384,1,128]{2,1,0:T(1,128)S(1)} async-done(((f32[384,1,128]{2,1,0:T(1,128)}), f32[384,1,128]{2,1,0:T(1,128)S(1)}, u32[]{:S(2)}, u32[]{:S(2)}) %all-to-all-start.7) | async-done | bytes 196640 | tf_op jit(solution)/shard_map/all_to_all | solution.py:126
  124.8 0.6 multiply_reduce_fusion.48
  125.4 0.2 multiply_reduce_fusion.39
  125.6 0.2 multiply_reduce_fusion.29
  125.8 0.2 multiply_reduce_fusion.19
  126.1 0.2 multiply_reduce_fusion.1
  126.3 0.2 multiply_reduce_fusion
  126.8 0.6 copy-done.2
  127.5 1.0 multiply_add_fusion
  128.5 0.6 convolution_bitcast_fusion.1
  129.1 0.8 copy.22
  129.9 6.2 all-to-all-start
  136.1 0.6 fusion.5
  136.7 0.8 copy.23
  137.5 11.3 %all-to-all-done = f32[3,128,128]{2,0,1:T(4,128)S(1)} async-done(((f32[3,128,128]{2,0,1:T(4,128)}), f32[3,128,128]{2,0,1:T(4,128)S(1)}, u32[]{:S(2)}, u32[]{:S(2)}) %all-to-all-start) | async-done | bytes 196640 | tf_op jit(solution)/shard_map/all_to_all | solution.py:103
  148.8 6.5 all-to-all-start.1
  155.3 0.1 reshape.102
  155.4 12.6 %all-to-all-done.1 = f32[3,128,128]{2,0,1:T(4,128)S(1)} async-done(((f32[3,128,128]{2,0,1:T(4,128)}), f32[3,128,128]{2,0,1:T(4,128)S(1)}, u32[]{:S(2)}, u32[]{:S(2)}) %all-to-all-start.1) | async-done | bytes 196640 | tf_op jit(solution)/shard_map/all_to_all | solution.py:104
  168.2 3.6 fusion.29
  171.8 3.6 fusion.27
  175.4 3.6 convolution_add_fusion.3
  179.0 3.6 convolution_subtract_fusion.5
  182.6 2.9 fusion.25
  185.5 3.6 convolution_subtract_fusion.4
  189.1 6.4 all-to-all-start.2
  195.6 2.9 fusion.23
  198.5 3.6 convolution_add_fusion.2
  202.2 5.8 all-to-all-done.2
  208.0 8.4 %all-to-all-start.3 = ((f32[384,1,128]{2,1,0:T(1,128)}), f32[384,1,128]{2,1,0:T(1,128)S(1)}, u32[]{:S(2)}, u32[]{:S(2)}) async-start(f32[384,1,128]{2,1,0:T(1,128)} %bitcast.67), calls=%async_computation.3 | async-start | bytes 393216 | tf_op jit(solution)/shard_map/all_to_all | solution.py:112
  216.4 0.8 pad_maximum_fusion
  217.2 1.3 collective-permute-start.3
  218.5 4.6 collective-permute-start.2
  223.1 0.6 fusion.150
  223.6 5.2 all-to-all-done.3
  228.9 1.2 fusion.7
  230.2 1.7 fusion.156
  231.9 582.4 %all-gather.3.cloned.1.call-done = f32[896,7,128]{2,1,0:T(8,128)} async-done(((f32[7,7,128]{2,1,0:T(8,128)}), f32[896,7,128]{2,1,0:T(8,128)}) %all-gather.3.cloned.1.call-update) | async-done | bytes 3211280 | tf_op jit(solution)/shard_map/all_gather | solution.py:12
  814.3 2.3 reduce_sum.499
  816.6 0.6 broadcast_multiply_fusion
  (35 shorter events, 0.6 us)
Async XLA Ops:
  7.2 0.9 copy-start
  9.4 30.0 %all-to-all-start.4 = ((f32[3,128,128]{2,0,1:T(4,128)}), f32[3,128,128]{2,0,1:T(4,128)S(1)}, u32[]{:S(2)}, u32[]{:S(2)}) async-start(f32[3,128,128]{2,0,1:T(4,128)} %copy.28), calls=%async_computation.4 | async-start | bytes 524288 | tf_op jit(solution)/shard_map/all_to_all | solution.py:115
  26.0 44.4 %copy-start.4 = (bf16[2,384,1,128]{3,1,2,0:T(8,128)(2,1)S(1)}, bf16[2,384,1,128]{3,1,2,0:T(8,128)(2,1)}, u32[]{:S(2)}) copy-start(bf16[2,384,1,128]{3,1,2,0:T(8,128)(2,1)} %param.6) | copy-start | bytes 589828
  39.4 20.2 %all-to-all-start.5 = ((f32[3,128,128]{2,0,1:T(4,128)}), f32[3,128,128]{2,0,1:T(4,128)S(1)}, u32[]{:S(2)}, u32[]{:S(2)}) async-start(f32[3,128,128]{2,0,1:T(4,128)} %copy.29), calls=%async_computation.5 | async-start | bytes 524288 | tf_op jit(solution)/shard_map/all_to_all | solution.py:116
  45.5 67.3 %collective-permute-start.1 = (bf16[3,128,128]{2,1,0:T(8,128)(2,1)}, bf16[3,128,128]{2,1,0:T(8,128)(2,1)S(1)}, u32[]{:S(2)}, u32[]{:S(2)}) collective-permute-start(bf16[3,128,128]{2,1,0:T(8,128)(2,1)} %param.4), channel_id=1, source_target_pairs={{4,0},{8,4},{12,8},{16,12},{20,16},{24,20},{28,24},{32,28},{36,32}... | collective-permute-start | bytes 294920 | tf_op jit(solution)/shard_map/ppermute | solution.py:28
  46.8 66.0 %collective-permute-start = (bf16[3,128,128]{2,1,0:T(8,128)(2,1)}, bf16[3,128,128]{2,1,0:T(8,128)(2,1)S(1)}, u32[]{:S(2)}, u32[]{:S(2)}) collective-permute-start(bf16[3,128,128]{2,1,0:T(8,128)(2,1)} %param.4), channel_id=1, source_target_pairs={{0,4},{4,8},{8,12},{12,16},{16,20},{20,24},{24,28},{28,32},{32,36}... | collective-permute-start | bytes 294920 | tf_op jit(solution)/shard_map/ppermute | solution.py:25
  70.5 42.4 %copy-start.1 = (bf16[3,128,128]{2,1,0:T(8,128)(2,1)S(1)}, bf16[3,128,128]{2,1,0:T(8,128)(2,1)}, u32[]{:S(2)}) copy-start(bf16[3,128,128]{2,1,0:T(8,128)(2,1)} %param.4) | copy-start | bytes 294916
  77.1 26.9 %all-to-all-start.6 = ((f32[384,1,128]{2,1,0:T(1,128)}), f32[384,1,128]{2,1,0:T(1,128)S(1)}, u32[]{:S(2)}, u32[]{:S(2)}) async-start(f32[384,1,128]{2,1,0:T(1,128)} %bitcast.79), calls=%async_computation.6 | async-start | bytes 393216 | tf_op jit(solution)/shard_map/all_to_all | solution.py:125
  104.0 20.8 %all-to-all-start.7 = ((f32[384,1,128]{2,1,0:T(1,128)}), f32[384,1,128]{2,1,0:T(1,128)S(1)}, u32[]{:S(2)}, u32[]{:S(2)}) async-start(f32[384,1,128]{2,1,0:T(1,128)} %bitcast.84), calls=%async_computation.7 | async-start | bytes 393216 | tf_op jit(solution)/shard_map/all_to_all | solution.py:126
  112.4 701.9 %all-gather.3.cloned.1.call-start = ((), (), s32[]{:S(2)}) async-start(), calls=%async_computation.8 | async-start | bytes 3698688 | tf_op jit(solution)/shard_map/all_gather | solution.py:12
  112.9 14.5 %copy-start.3 = (f32[7,7,128]{2,1,0:T(8,128)S(1)}, f32[7,7,128]{2,1,0:T(8,128)}, u32[]{:S(2)}) copy-start(f32[7,7,128]{2,1,0:T(8,128)} %param.5) | copy-start | bytes 75268
  126.8 0.6 copy-start.2
  129.9 18.9 %all-to-all-start = ((f32[3,128,128]{2,0,1:T(4,128)}), f32[3,128,128]{2,0,1:T(4,128)S(1)}, u32[]{:S(2)}, u32[]{:S(2)}) async-start(f32[3,128,128]{2,0,1:T(4,128)} %copy.22), calls=%async_computation | async-start | bytes 524288 | tf_op jit(solution)/shard_map/all_to_all | solution.py:103
  148.8 19.3 %all-to-all-start.1 = ((f32[3,128,128]{2,0,1:T(4,128)}), f32[3,128,128]{2,0,1:T(4,128)S(1)}, u32[]{:S(2)}, u32[]{:S(2)}) async-start(f32[3,128,128]{2,0,1:T(4,128)} %copy.23), calls=%async_computation.1 | async-start | bytes 524288 | tf_op jit(solution)/shard_map/all_to_all | solution.py:104
  189.1 18.9 %all-to-all-start.2 = ((f32[384,1,128]{2,1,0:T(1,128)}), f32[384,1,128]{2,1,0:T(1,128)S(1)}, u32[]{:S(2)}, u32[]{:S(2)}) async-start(f32[384,1,128]{2,1,0:T(1,128)} %bitcast.62), calls=%async_computation.2 | async-start | bytes 393216 | tf_op jit(solution)/shard_map/all_to_all | solution.py:111
  208.0 20.9 %all-to-all-start.3 = ((f32[384,1,128]{2,1,0:T(1,128)}), f32[384,1,128]{2,1,0:T(1,128)S(1)}, u32[]{:S(2)}, u32[]{:S(2)}) async-start(f32[384,1,128]{2,1,0:T(1,128)} %bitcast.67), calls=%async_computation.3 | async-start | bytes 393216 | tf_op jit(solution)/shard_map/all_to_all | solution.py:112
  217.2 12.9 %collective-permute-start.3 = (f32[3,128,128]{2,1,0:T(8,128)S(1)}, f32[3,128,128]{2,1,0:T(8,128)S(1)}, u32[]{:S(2)}, u32[]{:S(2)}) collective-permute-start(f32[3,128,128]{2,1,0:T(8,128)S(1)} %get-tuple-element.116), channel_id=1, source_target_pairs={{4,0},{8,4},{12,8},{16,12},{20,16},{24,20},{28,24},{32,28},{36,32}... | collective-permute-start | bytes 589832 | tf_op jit(solution)/shard_map/ppermute | solution.py:28
  218.5 11.6 %collective-permute-start.2 = (f32[3,128,128]{2,1,0:T(8,128)S(1)}, f32[3,128,128]{2,1,0:T(8,128)S(1)}, u32[]{:S(2)}, u32[]{:S(2)}) collective-permute-start(f32[3,128,128]{2,1,0:T(8,128)S(1)} %get-tuple-element.116), channel_id=1, source_target_pairs={{0,4},{4,8},{8,12},{12,16},{16,20},{20,24},{24,28},{28,32},{32,36}... | collective-permute-start | bytes 589832 | tf_op jit(solution)/shard_map/ppermute | solution.py:25
Sparse Core Ops, SparseCore 0:
  127.6 686.6 all-gather.2
